TPU v7x, 32 devices: a whole 2x2x4 slice. The times are simulated.
32 devices in a mesh: samp: 16 (over z, x, core), snp: 2 (over y).
Axes of the slice: x: 2, y: 2, z: 4, core: 2. Of those that a mesh axis runs over, the one named last changes fastest.
Arguments:
- genotypes: int32 [65536, 4096], P('samp', 'snp'), may hold values from 0 to 2, as said below
- allele_freq: float32 [4096], P('snp'), may hold values from 0.05 to 0.5
- snp_bins: int32 [4096], P('snp'), may hold values from 0 to 11, as said below
- probes: bfloat16 [64, 65536], P(None, 'samp'), may hold values from -6 to 6
- variances: float32 [13], replicated, may hold values from 0.1 to 1
Outputs:
- projected: float32 [65536, 768], P(('samp', 'snp'))
- combined: float32 [64, 65536], P(None, ('samp', 'snp'))
Inputs may be any that keep to these rules, and one draw needn't show every extreme that they name: `genotypes`: dosages 0, 1 or 2. `snp_bins`: every component has at least one SNP.
All inputs are finite; a program needn't handle non-finite values.
Results may differ from a plain program's by a relative error of at most 0.0065.
Values may be sent and summed in bfloat16 or wider, within the bound.
A program may use at most 192 MiB of HBM per device.

v0:
```python
import jax
import jax.numpy as jnp
from jax import lax
from jax.sharding import PartitionSpec as P

COMPONENTS = 12
CHUNKS = 4


def standardize(dosage_block, allele_freq):
    spread = jnp.sqrt(2.0 * allele_freq * (1.0 - allele_freq))
    return ((dosage_block.astype(jnp.float32) - 2.0 * allele_freq) / spread).astype(jnp.bfloat16)


def body(genotypes, allele_freq, snp_bins, probes, variances):
    groups = lax.axis_size("snp")
    me = lax.axis_index("snp")
    labels = jnp.arange(COMPONENTS, dtype=jnp.int32)
    onehot = (snp_bins[:, None] == labels[None, :]).astype(jnp.float32)
    counts = lax.psum(jnp.sum(onehot, 0), "snp")
    standard = standardize(genotypes, allele_freq)
    partial_scores = jnp.dot(probes, standard, preferred_element_type=jnp.float32)
    whole_rows = standard.shape[0] * lax.axis_size("samp")
    scores = lax.psum(partial_scores, "samp") / jnp.sqrt(jnp.float32(whole_rows))
    factor = jnp.sum(onehot * lax.rsqrt(counts)[None, :], 1)
    width = scores.shape[0]
    weights = (
        ((scores.T * factor[:, None])[:, None, :] * onehot[:, :, None])
        .reshape(snp_bins.shape[0], COMPONENTS * width)
        .astype(jnp.bfloat16)
    )
    own_rows = standard.shape[0] // groups
    piece = own_rows // CHUNKS

    def product(target, chunk):
        rows = lax.dynamic_slice_in_dim(standard, target * own_rows + chunk * piece, piece, 0)
        return jnp.dot(rows, weights, preferred_element_type=jnp.float32)

    got = [[] for _ in range(CHUNKS)]
    for shift in range(1, groups):
        ring = [(i, (i + shift) % groups) for i in range(groups)]
        for chunk in range(CHUNKS):
            sent = product(lax.rem(me + shift, groups), chunk).astype(jnp.bfloat16)
            got[chunk].append(lax.ppermute(sent, "snp", ring))
    blocks = []
    for chunk in range(CHUNKS):
        total = product(me, chunk)
        for term in got[chunk]:
            total = total + term.astype(jnp.float32)
        blocks.append(total)
    projected = jnp.concatenate(blocks, 0)
    stacked = projected.reshape(own_rows, COMPONENTS, width)
    own_probes = lax.dynamic_slice_in_dim(probes, me * own_rows, own_rows, 1).astype(jnp.float32)
    combined = (
        jnp.einsum("nmb,m->bn", stacked, variances[:COMPONENTS])
        + variances[COMPONENTS] * own_probes
    )
    return (projected, combined)


def solution(mesh):
    placed = (P("samp", "snp"), P("snp"), P("snp"), P(None, "samp"), P())
    return jax.shard_map(
        body,
        mesh=mesh,
        in_specs=placed,
        out_specs=(P(("samp", "snp"), None), P(None, ("samp", "snp"))),
        check_vma=False,
    )
```

profile of v0, /device:TPU:0, one launch (start us, length us, event | category | flops | bytes accessed | tf_op | source)
XLA Modules:
  0.0 278.8 jit_solution(911292419012415044)
XLA Ops:
  7.9 13.0 %divide_convert_fusion = bf16[4096,2048]{1,0:T(8,128)(2,1)S(1)} fusion(s32[4096,2048]{1,0:T(8,128)} %param.5, f32[2048]{0:T(1024)S(1)} %get-tuple-element.3, f32[2048]{0:T(1024)S(1)} %get-tuple-element.2), kind=kLoop, calls=%fused_computation | loop fusion | flops 33554432 | bytes 50348032 | tf_op jit(solution)/shard_map/convert_element_type | solution.py:12
  21.0 5.7 %copy-done = bf16[4096,2048]{1,0:T(8,128)(2,1)} copy-done((bf16[4096,2048]{1,0:T(8,128)(2,1)}, bf16[4096,2048]{1,0:T(8,128)(2,1)S(1)}, u32[]{:S(2)}) %copy-start) | copy-done | bytes 16777240
  26.7 3.9 %convolution_bitcast_fusion = f32[64,2048]{1,0:T(8,128)} fusion(bf16[64,4096]{1,0:T(8,128)(2,1)S(1)} %copy-done.2, bf16[4096,2048]{1,0:T(8,128)(2,1)S(1)} %divide_convert_fusion), kind=kOutput, calls=%fused_computation.5 | convolution fusion | flops 1073741824 | bytes 17825792 | tf_op jit(solution)/shard_map/dot_general | solution.py:22
  30.7 6.1 %psum.15 = f32[12]{0:T(128)S(1)} all-reduce(f32[12]{0:T(128)S(1)} %fusion.31), channel_id=1, replica_groups=mesh['samp'=16,'snp'=2] {'snp'}, use_global_device_ids=true, to_apply=%region_2.0 | all-reduce | flops 12 | bytes 96 | tf_op jit(solution)/shard_map/psum | solution.py:20
  37.5 86.6 %all-reduce.2.cloned.1.call-done = f32[64,2048]{1,0:T(8,128)} async-done(((f32[64,2048]{1,0:T(8,128)}), f32[64,2048]{1,0:T(8,128)}) %all-reduce.2.cloned.1.call-update) | async-done | bytes 524304 | tf_op jit(solution)/shard_map/psum | solution.py:24
  125.9 3.6 %fusion.18 = bf16[512,768]{1,0:T(8,128)(2,1)S(1)} fusion(bf16[2048,768]{0,1:T(8,128)(2,1)S(1)} %bitcast.25, bf16[4096,2048]{1,0:T(8,128)(2,1)} %copy-done, s32[]{:T(128)S(6)} %select_n.26), kind=kOutput, calls=%fused_computation.26 | convolution fusion | flops 1611005952 | bytes 6029316 | tf_op jit(solution)/shard_map/dot_general | solution.py:37
  129.5 1.5 collective-permute-start
  131.0 3.7 %fusion.21 = bf16[512,768]{1,0:T(8,128)(2,1)S(1)} fusion(bf16[2048,768]{0,1:T(8,128)(2,1)S(1)} %bitcast.26, bf16[4096,2048]{1,0:T(8,128)(2,1)} %copy-done, s32[]{:T(128)S(6)} %select_n.28), kind=kOutput, calls=%fused_computation.27 | convolution fusion | flops 1611005952 | bytes 6029316 | tf_op jit(solution)/shard_map/dot_general | solution.py:37
  134.8 1.1 collective-permute-start.1
  135.9 1.8 fusion.24
  138.7 1.8 fusion.27
  141.7 8.3 %collective-permute-done = bf16[512,768]{1,0:T(8,128)(2,1)S(1)} collective-permute-done((bf16[512,768]{1,0:T(8,128)(2,1)S(1)}, bf16[512,768]{1,0:T(8,128)(2,1)S(1)}, u32[]{:S(2)}, u32[]{:S(2)}) %collective-permute-start) | collective-permute-done | bytes 786464 | tf_op jit(solution)/shard_map/ppermute | solution.py:44
  150.0 1.8 convert_add_fusion.3
  151.8 15.0 %collective-permute-done.1 = bf16[512,768]{1,0:T(8,128)(2,1)S(1)} collective-permute-done((bf16[512,768]{1,0:T(8,128)(2,1)S(1)}, bf16[512,768]{1,0:T(8,128)(2,1)S(1)}, u32[]{:S(2)}, u32[]{:S(2)}) %collective-permute-start.1) | collective-permute-done | bytes 786464 | tf_op jit(solution)/shard_map/ppermute | solution.py:44
  166.9 1.8 convert_add_fusion.2
  168.7 15.0 %collective-permute-done.2 = bf16[512,768]{1,0:T(8,128)(2,1)S(1)} collective-permute-done((bf16[512,768]{1,0:T(8,128)(2,1)S(1)}, bf16[512,768]{1,0:T(8,128)(2,1)S(1)}, u32[]{:S(2)}, u32[]{:S(2)}) %collective-permute-start.2) | collective-permute-done | bytes 786464 | tf_op jit(solution)/shard_map/ppermute | solution.py:44
  183.7 1.8 convert_add_fusion.1
  185.5 14.4 %collective-permute-done.3 = bf16[512,768]{1,0:T(8,128)(2,1)S(1)} collective-permute-done((bf16[512,768]{1,0:T(8,128)(2,1)S(1)}, bf16[512,768]{1,0:T(8,128)(2,1)S(1)}, u32[]{:S(2)}, u32[]{:S(2)}) %collective-permute-start.3) | collective-permute-done | bytes 786464 | tf_op jit(solution)/shard_map/ppermute | solution.py:44
  200.0 2.1 convert_add_fusion
  202.0 2.9 %pad_maximum_fusion = f32[2048,768]{1,0:T(8,128)} fusion(f32[512,768]{1,0:T(8,128)S(1)} %convert_add_fusion, f32[512,768]{1,0:T(8,128)S(1)} %convert_add_fusion.1, f32[512,768]{1,0:T(8,128)S(1)} %convert_add_fusion.2, f32[512,768]{1,0:T(8,128)S(1)} %convert_add_fusion.3), kind=kLoop, calls=%fused_computation.3 | loop fusion | flops 4718592 | bytes 12582912 | tf_op jit(solution)/shard_map/concatenate | solution.py:51
  205.0 4.0 %copy.8 = bf16[2048,768]{0,1:T(8,128)(2,1)S(1)} copy(f32[2048,768]{1,0:T(8,128)} %pad_maximum_fusion) | data formatting | bytes 9437184 | tf_op jit(solution)/shard_map/concatenate | solution.py:51
  209.0 23.2 %fusion = f32[1,2048,64]{0,1,2:T(8,128)} fusion(bf16[2048,12,64]{0,2,1:T(8,128)(2,1)S(1)} %bitcast.24, f32[13]{0:T(128)S(1)} %copy-done.5), kind=kOutput, calls=%fused_computation.1 | convolution fusion | flops 3145728 | bytes 3670068 | tf_op jit(solution)/shard_map/nmb,m->bn/dot_general | solution.py:55
  232.1 38.3 %copy.10 = f32[1,2048,64]{1,2,0:T(8,128)S(1)} copy(f32[1,2048,64]{0,1,2:T(8,128)} %fusion) | data formatting | bytes 1048576 | tf_op jit(solution)/shard_map/nmb,m->bn/dot_general | solution.py:55
  270.5 1.5 bitcast_add_fusion
  (24 shorter events, 5.6 us)
Async XLA Ops:
  7.2 117.0 %all-reduce.2.cloned.1.call-start = ((), (), s32[]{:S(2)}) async-start(), calls=%async_computation | async-start | bytes 1048576 | tf_op jit(solution)/shard_map/psum | solution.py:24
  7.9 18.8 %copy-start.2 = (bf16[64,4096]{1,0:T(8,128)(2,1)S(1)}, bf16[64,4096]{1,0:T(8,128)(2,1)}, u32[]{:S(2)}) copy-start(bf16[64,4096]{1,0:T(8,128)(2,1)} %param.8) | copy-start | bytes 1572868
  20.9 5.7 %copy-start = (bf16[4096,2048]{1,0:T(8,128)(2,1)}, bf16[4096,2048]{1,0:T(8,128)(2,1)S(1)}, u32[]{:S(2)}) copy-start(bf16[4096,2048]{1,0:T(8,128)(2,1)S(1)} %divide_convert_fusion) | copy-start | bytes 50331652
  26.7 3.9 %copy-start.4 = (s32[2048]{0:T(1024)S(1)}, s32[2048]{0:T(1024)}, u32[]{:S(2)}) copy-start(s32[2048]{0:T(1024)} %param.7) | copy-start | bytes 24580
  26.7 10.3 %copy-start.5 = (f32[13]{0:T(128)S(1)}, f32[13]{0:T(128)}, u32[]{:S(2)}) copy-start(f32[13]{0:T(128)} %param.9) | copy-start | bytes 160
  125.9 9.9 %copy-start.1 = (bf16[4096,2048]{1,0:T(8,128)(2,1)S(1)}, bf16[4096,2048]{1,0:T(8,128)(2,1)}, u32[]{:S(2)}) copy-start(bf16[4096,2048]{1,0:T(8,128)(2,1)} %copy-done) | copy-start | bytes 50331652
  129.5 20.5 %collective-permute-start = (bf16[512,768]{1,0:T(8,128)(2,1)S(1)}, bf16[512,768]{1,0:T(8,128)(2,1)S(1)}, u32[]{:S(2)}, u32[]{:S(2)}) collective-permute-start(bf16[512,768]{1,0:T(8,128)(2,1)S(1)} %fusion.18), channel_id=1, source_target_pairs={{0,1},{1,0},{2,3},{3,2},{4,5},{5,4},{6,7},{7,6},{8,9},{9,8},{10,11... | collective-permute-start | bytes 2359304 | tf_op jit(solution)/shard_map/ppermute | solution.py:44
  134.8 32.1 %collective-permute-start.1 = (bf16[512,768]{1,0:T(8,128)(2,1)S(1)}, bf16[512,768]{1,0:T(8,128)(2,1)S(1)}, u32[]{:S(2)}, u32[]{:S(2)}) collective-permute-start(bf16[512,768]{1,0:T(8,128)(2,1)S(1)} %fusion.21), channel_id=1, source_target_pairs={{0,1},{1,0},{2,3},{3,2},{4,5},{5,4},{6,7},{7,6},{8,9},{9,8},{10,11... | collective-permute-start | bytes 2359304 | tf_op jit(solution)/shard_map/ppermute | solution.py:44
  137.7 46.0 %collective-permute-start.2 = (bf16[512,768]{1,0:T(8,128)(2,1)S(1)}, bf16[512,768]{1,0:T(8,128)(2,1)S(1)}, u32[]{:S(2)}, u32[]{:S(2)}) collective-permute-start(bf16[512,768]{1,0:T(8,128)(2,1)S(1)} %fusion.24), channel_id=1, source_target_pairs={{0,1},{1,0},{2,3},{3,2},{4,5},{5,4},{6,7},{7,6},{8,9},{9,8},{10,11... | collective-permute-start | bytes 2359304 | tf_op jit(solution)/shard_map/ppermute | solution.py:44
  140.6 59.4 %collective-permute-start.3 = (bf16[512,768]{1,0:T(8,128)(2,1)S(1)}, bf16[512,768]{1,0:T(8,128)(2,1)S(1)}, u32[]{:S(2)}, u32[]{:S(2)}) collective-permute-start(bf16[512,768]{1,0:T(8,128)(2,1)S(1)} %fusion.27), channel_id=1, source_target_pairs={{0,1},{1,0},{2,3},{3,2},{4,5},{5,4},{6,7},{7,6},{8,9},{9,8},{10,11... | collective-permute-start | bytes 2359304 | tf_op jit(solution)/shard_map/ppermute | solution.py:44
  232.1 38.3 %copy-start.3 = (bf16[64,4096]{1,0:T(8,128)(2,1)S(1)}, bf16[64,4096]{1,0:T(8,128)(2,1)}, u32[]{:S(2)}) copy-start(bf16[64,4096]{1,0:T(8,128)(2,1)} %param.8) | copy-start | bytes 1572868
Sparse Core Ops, SparseCore 0:
  30.7 93.4 all-reduce.1
where the time goes:
time: 280 us; the launch traced here: 279 us
  waiting for transfers between devices  139 us (50%)
  local copies, waits for them, and re-layouts  48.6 us (17%)
  matrix products  45.5 us (16%)
  other arithmetic  20.2 us (7%)
  between operations  14.2 us (5%)
  blocking collectives  6.08 us (2%)
  starting transfers between devices  4.81 us (2%)
    psum x1, waiting for transfers between devices, body(): lax.psum(partial_scores, 'samp') / jnp.sqrt(jnp.float32(whole_rows))  86.6 us
    ppermute x4, waiting for transfers between devices, body(): got[chunk].append(lax.ppermute(sent, 'snp', ring))  52.8 us
    dot_general x1, local copies, waits for them, and re-layouts, body(): jnp.einsum('nmb,m->bn', stacked, variances[:COMPONENTS])  38.3 us
    dot_general x1, matrix products, body(): jnp.einsum('nmb,m->bn', stacked, variances[:COMPONENTS])  23.2 us
    dot_general x8, matrix products, product(): return jnp.dot(rows, weights, preferred_element_type=jnp.float32)  18.4 us
    convert_element_type x1, other arithmetic, standardize(): ((dosage_block.astype(jnp.float32) - 2.0 * allele_freq) / spread).astype(...  13 us
    psum x1, blocking collectives, body(): counts = lax.psum(jnp.sum(onehot, 0), 'snp')  6.08 us
    unnamed x12, local copies, waits for them, and re-layouts  5.74 us
  transfers between devices with their start and end apart: 5, of which 5 were waited for; matrix products, arithmetic and copies ran while one was open for 5% of the time, Pallas kernels for 0%

commit v1 on v0

--- a/solution.py
+++ b/solution.py
@@ -21,7 +21,7 @@
     standard = standardize(genotypes, allele_freq)
     partial_scores = jnp.dot(probes, standard, preferred_element_type=jnp.float32)
     whole_rows = standard.shape[0] * lax.axis_size("samp")
-    scores = lax.psum(partial_scores, "samp") / jnp.sqrt(jnp.float32(whole_rows))
+    scores = lax.all_gather(partial_scores, "samp").sum(axis=0) / jnp.sqrt(jnp.float32(whole_rows))
     factor = jnp.sum(onehot * lax.rsqrt(counts)[None, :], 1)
     width = scores.shape[0]
     weights = (

time: 280 us -> 266 us (0.950)
  waiting for transfers between devices: 139 us -> 121 us
  other arithmetic: 20.2 us -> 23.1 us
    psum x1 -> x0, waiting for transfers between devices: 86.6 us -> none  [body(): lax.psum(partial_scores, 'samp') / jnp.sqrt(jnp.float32(whole_rows))]
    all_gather x0 -> x1, waiting for transfers between devices: none -> 70.2 us  [body(): lax.all_gather(partial_scores, 'samp').sum(axis=0)]
    reduce_sum x0 -> x1, other arithmetic: none -> 3.94 us  [body(): lax.all_gather(partial_scores, 'samp').sum(axis=0)]
    unnamed x12 -> x18, local copies, waits for them, and re-layouts: 5.74 us -> 5.76 us
  transfers between devices with their start and end apart: 5 -> 5, of which waited for: 5 -> 5; matrix products, arithmetic and copies ran while one was open for 5% -> 6% of each run, Pallas kernels for 0% -> 0%
where the time goes in v1:
time: 266 us; the launch traced here: 265 us
  waiting for transfers between devices  121 us (45%)
  local copies, waits for them, and re-layouts  48.7 us (18%)
  matrix products  47.1 us (18%)
  other arithmetic  23.1 us (9%)
  between operations  14.2 us (5%)
  blocking collectives  6.08 us (2%)
  starting transfers between devices  4.6 us (2%)
    all_gather x1, waiting for transfers between devices, body(): lax.all_gather(partial_scores, 'samp').sum(axis=0)  70.2 us
    ppermute x4, waiting for transfers between devices, body(): got[chunk].append(lax.ppermute(sent, 'snp', ring))  50.9 us
    dot_general x1, local copies, waits for them, and re-layouts, body(): jnp.einsum('nmb,m->bn', stacked, variances[:COMPONENTS])  38.3 us
    dot_general x1, matrix products, body(): jnp.einsum('nmb,m->bn', stacked, variances[:COMPONENTS])  23.1 us
    dot_general x8, matrix products, product(): return jnp.dot(rows, weights, preferred_element_type=jnp.float32)  20.1 us
    convert_element_type x1, other arithmetic, standardize(): ((dosage_block.astype(jnp.float32) - 2.0 * allele_freq) / spread).astype(...  13 us
    psum x1, blocking collectives, body(): counts = lax.psum(jnp.sum(onehot, 0), 'snp')  6.08 us
    unnamed x18, local copies, waits for them, and re-layouts  5.76 us
  transfers between devices with their start and end apart: 5, of which 5 were waited for; matrix products, arithmetic and copies ran while one was open for 6% of the time, Pallas kernels for 0%

profile of v1, /device:TPU:0, one launch (start us, length us, event | category | flops | bytes accessed | tf_op | source)
XLA Modules:
  0.0 264.9 jit_solution(3947269645151700390)
XLA Ops:
  7.9 13.0 %divide_convert_fusion = bf16[4096,2048]{1,0:T(8,128)(2,1)S(1)} fusion(s32[4096,2048]{1,0:T(8,128)} %param.5, f32[2048]{0:T(1024)S(1)} %get-tuple-element.3, f32[2048]{0:T(1024)S(1)} %get-tuple-element.2), kind=kLoop, calls=%fused_computation | loop fusion | flops 33554432 | bytes 50348032 | tf_op jit(solution)/shard_map/convert_element_type | solution.py:12
  21.0 5.7 %copy-done = bf16[4096,2048]{1,0:T(8,128)(2,1)} copy-done((bf16[4096,2048]{1,0:T(8,128)(2,1)}, bf16[4096,2048]{1,0:T(8,128)(2,1)S(1)}, u32[]{:S(2)}) %copy-start) | copy-done | bytes 16777240
  26.7 3.9 %convolution_bitcast_fusion = f32[64,2048]{1,0:T(8,128)} fusion(bf16[64,4096]{1,0:T(8,128)(2,1)S(1)} %copy-done.1, bf16[4096,2048]{1,0:T(8,128)(2,1)S(1)} %divide_convert_fusion), kind=kOutput, calls=%fused_computation.5 | convolution fusion | flops 1073741824 | bytes 17825792 | tf_op jit(solution)/shard_map/dot_general | solution.py:22
  30.7 6.1 %psum.7 = f32[12]{0:T(128)S(1)} all-reduce(f32[12]{0:T(128)S(1)} %fusion.31), channel_id=1, replica_groups=mesh['samp'=16,'snp'=2] {'snp'}, use_global_device_ids=true, to_apply=%region_2.0 | all-reduce | flops 12 | bytes 96 | tf_op jit(solution)/shard_map/psum | solution.py:20
  37.5 70.2 %all-gather.3.cloned.1.call-done = f32[1024,2048]{1,0:T(8,128)} async-done(((f32[64,2048]{1,0:T(8,128)}), f32[1024,2048]{1,0:T(8,128)}) %all-gather.3.cloned.1.call-update) | async-done | bytes 8388624 | tf_op jit(solution)/shard_map/all_gather | solution.py:24
  107.7 3.9 %reduce_sum.27 = f32[64,2048]{1,0:T(8,128)S(1)} reduce(f32[16,64,2048]{2,1,0:T(8,128)} %bitcast.28, f32[]{:T(128)} %constant.31.clone.1), dimensions={0}, to_apply=%region_0.0 | reduce | flops 1966080 | bytes 8912900 | tf_op jit(solution)/shard_map/reduce_sum | solution.py:24
  112.5 3.6 %fusion.18 = bf16[512,768]{1,0:T(8,128)(2,1)S(1)} fusion(bf16[2048,768]{0,1:T(8,128)(2,1)S(1)} %bitcast.29, bf16[4096,2048]{1,0:T(8,128)(2,1)} %copy-done, s32[]{:T(128)S(6)} %select_n.26), kind=kOutput, calls=%fused_computation.26 | convolution fusion | flops 1611005952 | bytes 6029316 | tf_op jit(solution)/shard_map/dot_general | solution.py:37
  116.0 1.5 collective-permute-start
  117.6 3.4 %fusion.21 = bf16[512,768]{1,0:T(8,128)(2,1)S(1)} fusion(bf16[2048,768]{0,1:T(8,128)(2,1)S(1)} %bitcast.30, bf16[4096,2048]{1,0:T(8,128)(2,1)} %copy-done, s32[]{:T(128)S(6)} %select_n.28), kind=kOutput, calls=%fused_computation.27 | convolution fusion | flops 1611005952 | bytes 6029316 | tf_op jit(solution)/shard_map/dot_general | solution.py:37
  121.9 3.8 %fusion.24 = bf16[512,768]{1,0:T(8,128)(2,1)S(1)} fusion(bf16[2048,768]{0,1:T(8,128)(2,1)S(1)} %bitcast.31, bf16[4096,2048]{1,0:T(8,128)(2,1)} %copy-done, s32[]{:T(128)S(6)} %select_n.30), kind=kOutput, calls=%fused_computation.28 | convolution fusion | flops 1611005952 | bytes 6029316 | tf_op jit(solution)/shard_map/dot_general | solution.py:37
  126.6 1.8 fusion.27
  129.7 6.8 %collective-permute-done = bf16[512,768]{1,0:T(8,128)(2,1)S(1)} collective-permute-done((bf16[512,768]{1,0:T(8,128)(2,1)S(1)}, bf16[512,768]{1,0:T(8,128)(2,1)S(1)}, u32[]{:S(2)}, u32[]{:S(2)}) %collective-permute-start) | collective-permute-done | bytes 786464 | tf_op jit(solution)/shard_map/ppermute | solution.py:44
  136.5 1.8 convert_add_fusion.3
  138.4 15.0 %collective-permute-done.1 = bf16[512,768]{1,0:T(8,128)(2,1)S(1)} collective-permute-done((bf16[512,768]{1,0:T(8,128)(2,1)S(1)}, bf16[512,768]{1,0:T(8,128)(2,1)S(1)}, u32[]{:S(2)}, u32[]{:S(2)}) %collective-permute-start.1) | collective-permute-done | bytes 786464 | tf_op jit(solution)/shard_map/ppermute | solution.py:44
  153.4 1.8 convert_add_fusion.2
  155.2 15.0 %collective-permute-done.2 = bf16[512,768]{1,0:T(8,128)(2,1)S(1)} collective-permute-done((bf16[512,768]{1,0:T(8,128)(2,1)S(1)}, bf16[512,768]{1,0:T(8,128)(2,1)S(1)}, u32[]{:S(2)}, u32[]{:S(2)}) %collective-permute-start.2) | collective-permute-done | bytes 786464 | tf_op jit(solution)/shard_map/ppermute | solution.py:44
  170.2 2.1 convert_add_fusion.1
  172.3 14.1 %collective-permute-done.3 = bf16[512,768]{1,0:T(8,128)(2,1)S(1)} collective-permute-done((bf16[512,768]{1,0:T(8,128)(2,1)S(1)}, bf16[512,768]{1,0:T(8,128)(2,1)S(1)}, u32[]{:S(2)}, u32[]{:S(2)}) %collective-permute-start.3) | collective-permute-done | bytes 786464 | tf_op jit(solution)/shard_map/ppermute | solution.py:44
  186.4 1.8 convert_add_fusion
  188.2 2.9 %pad_maximum_fusion = f32[2048,768]{1,0:T(8,128)} fusion(f32[512,768]{1,0:T(8,128)S(1)} %convert_add_fusion, f32[512,768]{1,0:T(8,128)S(1)} %convert_add_fusion.1, f32[512,768]{1,0:T(8,128)S(1)} %convert_add_fusion.2, f32[512,768]{1,0:T(8,128)S(1)} %convert_add_fusion.3), kind=kLoop, calls=%fused_computation.3 | loop fusion | flops 4718592 | bytes 12582912 | tf_op jit(solution)/shard_map/concatenate | solution.py:51
  191.1 4.0 %copy.8 = bf16[2048,768]{0,1:T(8,128)(2,1)S(1)} copy(f32[2048,768]{1,0:T(8,128)} %pad_maximum_fusion) | data formatting | bytes 9437184 | tf_op jit(solution)/shard_map/concatenate | solution.py:51
  195.1 23.1 %fusion = f32[1,2048,64]{0,1,2:T(8,128)} fusion(bf16[2048,12,64]{0,2,1:T(8,128)(2,1)S(1)} %bitcast.27, f32[13]{0:T(128)S(1)} %copy-done.4), kind=kOutput, calls=%fused_computation.1 | convolution fusion | flops 3145728 | bytes 3670068 | tf_op jit(solution)/shard_map/nmb,m->bn/dot_general | solution.py:55
  218.3 38.3 %copy.10 = f32[1,2048,64]{1,2,0:T(8,128)S(1)} copy(f32[1,2048,64]{0,1,2:T(8,128)} %fusion) | data formatting | bytes 1048576 | tf_op jit(solution)/shard_map/nmb,m->bn/dot_general | solution.py:55
  256.6 1.5 bitcast_add_fusion
  (32 shorter events, 5.4 us)
Async XLA Ops:
  7.2 100.6 %all-gather.3.cloned.1.call-start = ((), (), s32[]{:S(2)}) async-start(), calls=%async_computation | async-start | bytes 8912896 | tf_op jit(solution)/shard_map/all_gather | solution.py:24
  7.9 18.8 %copy-start.1 = (bf16[64,4096]{1,0:T(8,128)(2,1)S(1)}, bf16[64,4096]{1,0:T(8,128)(2,1)}, u32[]{:S(2)}) copy-start(bf16[64,4096]{1,0:T(8,128)(2,1)} %param.8) | copy-start | bytes 1572868
  20.9 5.7 %copy-start = (bf16[4096,2048]{1,0:T(8,128)(2,1)}, bf16[4096,2048]{1,0:T(8,128)(2,1)S(1)}, u32[]{:S(2)}) copy-start(bf16[4096,2048]{1,0:T(8,128)(2,1)S(1)} %divide_convert_fusion) | copy-start | bytes 50331652
  26.7 3.9 %copy-start.3 = (s32[2048]{0:T(1024)S(1)}, s32[2048]{0:T(1024)}, u32[]{:S(2)}) copy-start(s32[2048]{0:T(1024)} %param.7) | copy-start | bytes 24580
  26.7 10.1 %copy-start.4 = (f32[13]{0:T(128)S(1)}, f32[13]{0:T(128)}, u32[]{:S(2)}) copy-start(f32[13]{0:T(128)} %param.9) | copy-start | bytes 160
  112.4 14.2 %slice-start = ((s8[16777216]{0:T(1024)(128)(4,1)}), s8[4194304]{0:T(1024)(128)(4,1)S(1)}, s32[]{:S(2)}) async-start(s8[16777216]{0:T(1024)(128)(4,1)} %bitcast.25), calls=%async_computation.1 | async-start | bytes 8388608
  112.4 14.2 %slice-start.1 = ((s8[16777216]{0:T(1024)(128)(4,1)}), s8[4194304]{0:T(1024)(128)(4,1)S(1)}, s32[]{:S(2)}) async-start(s8[16777216]{0:T(1024)(128)(4,1)} %bitcast.25), calls=%async_computation.2 | async-start | bytes 8388608
  116.0 10.6 %slice-start.2 = ((s8[16777216]{0:T(1024)(128)(4,1)}), s8[4194304]{0:T(1024)(128)(4,1)S(1)}, s32[]{:S(2)}) async-start(s8[16777216]{0:T(1024)(128)(4,1)} %bitcast.25), calls=%async_computation.3 | async-start | bytes 8388608
  116.0 20.5 %collective-permute-start = (bf16[512,768]{1,0:T(8,128)(2,1)S(1)}, bf16[512,768]{1,0:T(8,128)(2,1)S(1)}, u32[]{:S(2)}, u32[]{:S(2)}) collective-permute-start(bf16[512,768]{1,0:T(8,128)(2,1)S(1)} %fusion.18), channel_id=1, source_target_pairs={{0,1},{1,0},{2,3},{3,2},{4,5},{5,4},{6,7},{7,6},{8,9},{9,8},{10,11... | collective-permute-start | bytes 2359304 | tf_op jit(solution)/shard_map/ppermute | solution.py:44
  121.0 5.6 %slice-start.3 = ((s8[16777216]{0:T(1024)(128)(4,1)}), s8[4194304]{0:T(1024)(128)(4,1)S(1)}, s32[]{:S(2)}) async-start(s8[16777216]{0:T(1024)(128)(4,1)} %bitcast.25), calls=%async_computation.4 | async-start | bytes 8388608
  121.0 32.4 %collective-permute-start.1 = (bf16[512,768]{1,0:T(8,128)(2,1)S(1)}, bf16[512,768]{1,0:T(8,128)(2,1)S(1)}, u32[]{:S(2)}, u32[]{:S(2)}) collective-permute-start(bf16[512,768]{1,0:T(8,128)(2,1)S(1)} %fusion.21), channel_id=1, source_target_pairs={{0,1},{1,0},{2,3},{3,2},{4,5},{5,4},{6,7},{7,6},{8,9},{9,8},{10,11... | collective-permute-start | bytes 2359304 | tf_op jit(solution)/shard_map/ppermute | solution.py:44
  125.7 44.5 %collective-permute-start.2 = (bf16[512,768]{1,0:T(8,128)(2,1)S(1)}, bf16[512,768]{1,0:T(8,128)(2,1)S(1)}, u32[]{:S(2)}, u32[]{:S(2)}) collective-permute-start(bf16[512,768]{1,0:T(8,128)(2,1)S(1)} %fusion.24), channel_id=1, source_target_pairs={{0,1},{1,0},{2,3},{3,2},{4,5},{5,4},{6,7},{7,6},{8,9},{9,8},{10,11... | collective-permute-start | bytes 2359304 | tf_op jit(solution)/shard_map/ppermute | solution.py:44
  128.5 57.9 %collective-permute-start.3 = (bf16[512,768]{1,0:T(8,128)(2,1)S(1)}, bf16[512,768]{1,0:T(8,128)(2,1)S(1)}, u32[]{:S(2)}, u32[]{:S(2)}) collective-permute-start(bf16[512,768]{1,0:T(8,128)(2,1)S(1)} %fusion.27), channel_id=1, source_target_pairs={{0,1},{1,0},{2,3},{3,2},{4,5},{5,4},{6,7},{7,6},{8,9},{9,8},{10,11... | collective-permute-start | bytes 2359304 | tf_op jit(solution)/shard_map/ppermute | solution.py:44
  218.3 38.3 %copy-start.2 = (bf16[64,4096]{1,0:T(8,128)(2,1)S(1)}, bf16[64,4096]{1,0:T(8,128)(2,1)}, u32[]{:S(2)}) copy-start(bf16[64,4096]{1,0:T(8,128)(2,1)} %param.8) | copy-start | bytes 1572868
Sparse Core Ops, SparseCore 0:
  30.7 77.0 all-gather.2
